TPU v7x, 256 devices: a whole 4x4x8 slice. The times are simulated.
256 devices in a mesh: occ: 32 (over z, y), va: 2 (over x_hi), vb: 4 (over x_lo, core).
Axes of the slice: x: 4 (x_hi: 2, x_lo: 2; x = x_hi * 2 + x_lo), y: 4, z: 8, core: 2. Of those that a mesh axis runs over, the one named last changes fastest.
Arguments:
- aux_factors: bfloat16 [32, 1024, 2048], P('occ', ('vb', 'va')), may hold values from -0.59765625 to 0.59765625
- occ_energy: float32 [32], replicated, may hold values from -2 to -0.5
- vir_energy: float32 [1024], replicated, may hold values from 0.5 to 3
- occ_index: int32 [32], replicated, may hold values from 0 to 31, each once
- vir_index: int32 [1024], replicated, may hold values from 0 to 1023, each once
Outputs:
- gamma_aux: float32 [32, 1024, 2048], P('occ', ('vb', 'va'))
Inputs may be any that keep to these rules, and one draw needn't show every extreme that they name: `occ_index`: each occupied table row appears exactly once. `vir_index`: each virtual table row appears exactly once.
All inputs are finite; a program needn't handle non-finite values.
Results may differ from a plain program's by a relative error of at most 0.0017.
Values may be sent and summed in bfloat16 or wider, within the bound.
A program may use at most 64 MiB of HBM per device.

v0:
```python
import jax
import jax.numpy as jnp
from jax import lax
from jax.sharding import PartitionSpec as P

STEPS = 4


def passed_along(block, axis, distance):
    devices = range(lax.axis_size(axis))
    route = [((i - distance) % len(devices), i) for i in devices]
    return lax.ppermute(block, axis, route)


def lookup(indices, energies):
    positions = jnp.arange(energies.shape[0], dtype=jnp.int32)
    matches = indices[:, None] == positions[None, :]
    return jnp.sum(jnp.where(matches, energies[None, :], 0.0), axis=1)


def per_device(aux_factors, occ_energy, vir_energy, occ_index, vir_index):
    va_count = lax.axis_size("va")
    vb_count = lax.axis_size("vb")
    occ_count = lax.axis_size("occ")
    va_rank = lax.axis_index("va")
    vb_rank = lax.axis_index("vb")
    occ_rank = lax.axis_index("occ")
    occ_rows, block_width, aux_width = aux_factors.shape
    vir_width = vir_index.shape[0]
    row_count = vb_count * block_width
    row_index = lax.dynamic_index_in_dim(
        vir_index.reshape(vb_count, va_count, block_width), va_rank, 1, False
    ).reshape(row_count)
    col_index = lax.dynamic_index_in_dim(
        vir_index.reshape(vb_count, vir_width // vb_count), vb_rank, 0, False
    )
    row_energy = lookup(row_index, vir_energy)
    col_energy = lookup(col_index, vir_energy)

    def block_energy(block_id):
        return lookup(
            lax.dynamic_slice_in_dim(occ_index, block_id * occ_rows, occ_rows), occ_energy
        )

    own_energy = block_energy(occ_rank)
    own_columns = lax.all_gather(aux_factors, "va", axis=1, tiled=True)
    own_rows = lax.all_gather(aux_factors, "vb", axis=1, tiled=True)
    gradient = jnp.zeros((occ_rows, row_count, aux_width), jnp.float32)
    far_columns = own_columns
    far_rows = own_rows
    for distance in range(STEPS):
        if distance > 0:
            far_columns, far_rows = passed_along((far_columns, far_rows), "occ", 1)
        far_block = (occ_rank - distance + occ_count) % occ_count
        kernel = jnp.einsum(
            "iap,jbp->iajb", own_rows, far_columns, preferred_element_type=jnp.float32
        )
        swapped = jnp.einsum(
            "ibp,jap->iajb", own_columns, far_rows, preferred_element_type=jnp.float32
        )
        energy_gap = (
            own_energy[:, None, None, None]
            + block_energy(far_block)[None, None, :, None]
            - row_energy[None, :, None, None]
            - col_energy[None, None, None, :]
        )
        weights = ((2.0 * kernel - swapped) / energy_gap).astype(jnp.bfloat16)
        gradient = gradient + jnp.einsum(
            "iajb,jbp->iap", weights, far_columns, preferred_element_type=jnp.float32
        )
    return lax.psum_scatter(gradient, "vb", scatter_dimension=1, tiled=True)


def solution(mesh):
    return jax.shard_map(
        per_device,
        mesh=mesh,
        in_specs=(P("occ", ("vb", "va"), None), P(), P(), P(), P()),
        out_specs=P("occ", ("vb", "va"), None),
        check_vma=False,
    )
```

profile of v0, /device:TPU:96, one launch (start us, length us, event | category | flops | bytes accessed | tf_op | source)
XLA Modules:
  0.0 326.7 jit_solution(3531416720527127044)
XLA Ops:
  7.4 0.0 all-gather.3.cloned.1.call-start
  7.4 0.7 all-gather.3.cloned.1.call-update
  8.1 0.0 all-gather.5.cloned.1.call-start
  8.1 35.2 %all-gather.3.cloned.1.call-done = bf16[1,512,2048]{2,1,0:T(8,128)(2,1)} async-done(((bf16[1,128,2048]{2,1,0:T(8,128)(2,1)}), bf16[1,512,2048]{2,1,0:T(8,128)(2,1)}) %all-gather.3.cloned.1.call-update) | async-done | bytes 2097168 | tf_op jit(solution)/shard_map/all_gather | solution.py:47
  43.4 1.5 collective-permute-start.1
  44.9 0.0 all-gather.5.cloned.1.call-update
  44.9 0.0 reduce-scatter.2.cloned.1.call-start
  44.9 48.8 %collective-permute-done.1 = bf16[1,512,2048]{2,1,0:T(8,128)(2,1)} collective-permute-done((bf16[1,512,2048]{2,1,0:T(8,128)(2,1)}, bf16[1,512,2048]{2,1,0:T(8,128)(2,1)}, u32[]{:S(2)}, u32[]{:S(2)}) %collective-permute-start.1) | collective-permute-done | bytes 2097184 | tf_op jit(solution)/shard_map/ppermute | solution.py:12
  93.8 0.0 collective-permute-start.3
  93.8 0.0 all-gather.5.cloned.1.call-done
  93.8 0.9 collective-permute-start
  94.7 71.1 %collective-permute-done = bf16[1,256,2048]{2,1,0:T(8,128)(2,1)S(1)} collective-permute-done((bf16[1,256,2048]{2,1,0:T(8,128)(2,1)}, bf16[1,256,2048]{2,1,0:T(8,128)(2,1)S(1)}, u32[]{:S(2)}, u32[]{:S(2)}) %collective-permute-start) | collective-permute-done | bytes 1048608 | tf_op jit(solution)/shard_map/ppermute | solution.py:12
  165.8 0.0 copy-start.2
  165.8 0.0 collective-permute-start.2
  165.8 1.6 fusion.115
  167.3 4.7 %fusion.110 = (f32[]{:T(128)}, f32[]{:T(128)}, f32[]{:T(128)}, f32[]{:T(128)}, f32[]{:T(128)}) fusion(f32[32]{0:T(128)} %param.6, s32[]{:T(128)} %bitcast.15, s32[]{:T(128)} %bitcast.9, s32[]{:T(128)} %bitcast.3, s32[]{:T(128)} %bitcast.2, s32[]{:T(128)} %bitcast.12), kind=kLoop, calls=%fused_computation.75 | loop fusion | flops 475 | bytes 168 | tf_op jit(solution)/shard_map/reduce_sum | solution.py:18
  177.1 0.7 reshape.173
  177.8 0.7 constant_dynamic-slice_fusion.1
  178.5 1.0 select_reduce_fusion
  179.5 0.0 collective-permute-done.3
  179.5 0.1 collective-permute-start.5
  179.6 0.9 select_reduce_fusion.1
  180.5 13.6 %collective-permute-done.2 = bf16[1,256,2048]{2,1,0:T(8,128)(2,1)} collective-permute-done((bf16[1,256,2048]{2,1,0:T(8,128)(2,1)S(1)}, bf16[1,256,2048]{2,1,0:T(8,128)(2,1)}, u32[]{:S(2)}, u32[]{:S(2)}) %collective-permute-start.2) | collective-permute-done | bytes 1048608 | tf_op jit(solution)/shard_map/ppermute | solution.py:12
  194.1 0.0 collective-permute-start.4
  194.1 0.0 copy-done.2
  194.1 0.0 copy-start.1
  194.1 6.7 %fusion.65 = f32[512,2048]{1,0:T(8,128)} fusion(bf16[1,256,2048]{2,1,0:T(8,128)(2,1)} %all-gather.5.cloned.1.call-done, bf16[1,512,2048]{2,1,0:T(8,128)(2,1)} %all-gather.3.cloned.1.call-done, f32[256]{0:T(256)S(1)} %select_reduce_fusion.1, f32[512]{0:T(512)S(1)} %get-tuple-element.13), kind=kOutput, calls=%fused_computation.38 | convolution fusion | flops 1074397184 | bytes 7343104 | tf_op jit(solution)/shard_map/iajb,jbp->iap/dot_general | solution.py:68
  200.8 0.0 copy-done.1
  200.8 0.0 copy-start
  200.8 3.3 %fusion.4 = f32[512,256]{1,0:T(8,128)} fusion(bf16[1,512,2048]{2,1,0:T(8,128)(2,1)} %collective-permute-done.1, bf16[1,256,2048]{2,1,0:T(8,128)(2,1)S(1)} %copy-done.1), kind=kOutput, calls=%fused_computation.5 | convolution fusion | flops 536870912 | bytes 3670016 | tf_op jit(solution)/shard_map/ibp,jap->iajb/dot_general | solution.py:58
  204.2 0.0 copy-done
  204.2 6.0 %fusion.54 = f32[512,2048]{1,0:T(8,128)} fusion(f32[512,256]{1,0:T(8,128)} %fusion.4, bf16[1,512,2048]{2,1,0:T(8,128)(2,1)S(1)} %copy-done, bf16[1,256,2048]{2,1,0:T(8,128)(2,1)} %copy-done.2, f32[512]{0:T(512)S(1)} %get-tuple-element.12, f32[256]{0:T(256)S(1)} %select_reduce_fusion.1), kind=kOutput, calls=%fused_computation.30 | convolution fusion | flops 1074397184 | bytes 7867392 | tf_op jit(solution)/shard_map/iajb,jbp->iap/dot_general | solution.py:68
  210.2 3.1 fusion.2
  213.3 6.0 %fusion.51 = f32[512,2048]{1,0:T(8,128)} fusion(f32[512,256]{1,0:T(8,128)} %fusion.2, bf16[1,512,2048]{2,1,0:T(8,128)(2,1)S(1)} %copy-done, bf16[1,256,2048]{2,1,0:T(8,128)(2,1)} %collective-permute-done.2, f32[512]{0:T(512)S(1)} %get-tuple-element.11, f32[256]{0:T(256)S(1)} %select_reduce_fusion.1), kind=kOutput, calls=%fused_computation.29 | convolution fusion | flops 1074397184 | bytes 7867392 | tf_op jit(solution)/shard_map/iajb,jbp->iap/dot_general | solution.py:68
  219.3 19.7 %collective-permute-done.5 = bf16[1,512,2048]{2,1,0:T(8,128)(2,1)} collective-permute-done((bf16[1,512,2048]{2,1,0:T(8,128)(2,1)}, bf16[1,512,2048]{2,1,0:T(8,128)(2,1)}, u32[]{:S(2)}, u32[]{:S(2)}) %collective-permute-start.5) | collective-permute-done | bytes 2097184 | tf_op jit(solution)/shard_map/ppermute | solution.py:12
  239.0 3.1 fusion
  242.2 17.1 %collective-permute-done.4 = bf16[1,256,2048]{2,1,0:T(8,128)(2,1)} collective-permute-done((bf16[1,256,2048]{2,1,0:T(8,128)(2,1)}, bf16[1,256,2048]{2,1,0:T(8,128)(2,1)}, u32[]{:S(2)}, u32[]{:S(2)}) %collective-permute-start.4) | collective-permute-done | bytes 1048608 | tf_op jit(solution)/shard_map/ppermute | solution.py:12
  259.2 9.8 %add_bitcast_fusion = f32[1,512,2048]{2,1,0:T(8,128)} fusion(f32[512,2048]{1,0:T(8,128)} %fusion.51, f32[512,2048]{1,0:T(8,128)} %fusion.65, f32[512,2048]{1,0:T(8,128)} %fusion.54, bf16[1,256,2048]{2,1,0:T(8,128)(2,1)} %collective-permute-done.4, f32[512,256]{1,0:T(8,128)} %fusion, bf16[1,512,2048]{2,1,0:T(8,128)(2,1)S(1)} %copy-done, ...), kind=kOutput, calls=%fused_computation | convolution fusion | flops 1077542912 | bytes 20450304 | tf_op jit(solution)/shard_map/iajb,jbp->iap/dot_general | solution.py:68
  269.0 0.0 reduce-scatter.2.cloned.1.call-update
  269.1 50.2 %reduce-scatter.2.cloned.1.call-done = f32[1,128,2048]{2,1,0:T(8,128)} async-done(((f32[1,512,2048]{2,1,0:T(8,128)}), f32[1,128,2048]{2,1,0:T(8,128)}) %reduce-scatter.2.cloned.1.call-update) | async-done | bytes 1048592 | tf_op jit(solution)/shard_map/reduce_scatter | solution.py:71
  (2 shorter events, 0.0 us)
Async XLA Ops:
  7.4 36.0 %all-gather.3.cloned.1.call-start = ((), (), s32[]{:S(2)}) async-start(), calls=%async_computation.1 | async-start | bytes 2621440 | tf_op jit(solution)/shard_map/all_gather | solution.py:47
  8.1 85.7 %all-gather.5.cloned.1.call-start = ((), (), s32[]{:S(2)}) async-start(), calls=%async_computation.2 | async-start | bytes 1572864 | tf_op jit(solution)/shard_map/all_gather | solution.py:46
  43.4 50.4 %collective-permute-start.1 = (bf16[1,512,2048]{2,1,0:T(8,128)(2,1)}, bf16[1,512,2048]{2,1,0:T(8,128)(2,1)}, u32[]{:S(2)}, u32[]{:S(2)}) collective-permute-start(bf16[1,512,2048]{2,1,0:T(8,128)(2,1)} %all-gather.3.cloned.1.call-done), channel_id=1, source_target_pairs={{248,0},{0,8},{8,16},{16,24},{24,32},{32,40},{40,48},{48,56},{56,6... | collective-permute-start | bytes 6291464 | tf_op jit(solution)/shard_map/ppermute | solution.py:12
  44.9 274.4 %reduce-scatter.2.cloned.1.call-start = ((), (), s32[]{:S(2)}) async-start(), calls=%async_computation.3 | async-start | bytes 5242880 | tf_op jit(solution)/shard_map/reduce_scatter | solution.py:71
  93.8 85.7 %collective-permute-start.3 = (bf16[1,512,2048]{2,1,0:T(8,128)(2,1)}, bf16[1,512,2048]{2,1,0:T(8,128)(2,1)}, u32[]{:S(2)}, u32[]{:S(2)}) collective-permute-start(bf16[1,512,2048]{2,1,0:T(8,128)(2,1)} %collective-permute-done.1), channel_id=1, source_target_pairs={{248,0},{0,8},{8,16},{16,24},{24,32},{32,40},{40,48},{48,56},{56,6... | collective-permute-start | bytes 6291464 | tf_op jit(solution)/shard_map/ppermute | solution.py:12
  93.8 72.0 %collective-permute-start = (bf16[1,256,2048]{2,1,0:T(8,128)(2,1)}, bf16[1,256,2048]{2,1,0:T(8,128)(2,1)S(1)}, u32[]{:S(2)}, u32[]{:S(2)}) collective-permute-start(bf16[1,256,2048]{2,1,0:T(8,128)(2,1)} %all-gather.5.cloned.1.call-done), channel_id=1, source_target_pairs={{248,0},{0,8},{8,16},{16,24},{24,32},{32,40},{40,48},{48,56},{56,6... | collective-permute-start | bytes 3145736 | tf_op jit(solution)/shard_map/ppermute | solution.py:12
  165.8 28.3 %copy-start.2 = (bf16[1,256,2048]{2,1,0:T(8,128)(2,1)}, bf16[1,256,2048]{2,1,0:T(8,128)(2,1)S(1)}, u32[]{:S(2)}) copy-start(bf16[1,256,2048]{2,1,0:T(8,128)(2,1)S(1)} %collective-permute-done) | copy-start | bytes 3145732
  165.8 28.3 %collective-permute-start.2 = (bf16[1,256,2048]{2,1,0:T(8,128)(2,1)S(1)}, bf16[1,256,2048]{2,1,0:T(8,128)(2,1)}, u32[]{:S(2)}, u32[]{:S(2)}) collective-permute-start(bf16[1,256,2048]{2,1,0:T(8,128)(2,1)S(1)} %collective-permute-done), channel_id=1, source_target_pairs={{248,0},{0,8},{8,16},{16,24},{24,32},{32,40},{40,48},{48,56},{56,6... | collective-permute-start | bytes 3145736 | tf_op jit(solution)/shard_map/ppermute | solution.py:12
  179.5 59.5 %collective-permute-start.5 = (bf16[1,512,2048]{2,1,0:T(8,128)(2,1)}, bf16[1,512,2048]{2,1,0:T(8,128)(2,1)}, u32[]{:S(2)}, u32[]{:S(2)}) collective-permute-start(bf16[1,512,2048]{2,1,0:T(8,128)(2,1)} %collective-permute-done.3), channel_id=1, source_target_pairs={{248,0},{0,8},{8,16},{16,24},{24,32},{32,40},{40,48},{48,56},{56,6... | collective-permute-start | bytes 6291464 | tf_op jit(solution)/shard_map/ppermute | solution.py:12
  194.1 65.1 %collective-permute-start.4 = (bf16[1,256,2048]{2,1,0:T(8,128)(2,1)}, bf16[1,256,2048]{2,1,0:T(8,128)(2,1)}, u32[]{:S(2)}, u32[]{:S(2)}) collective-permute-start(bf16[1,256,2048]{2,1,0:T(8,128)(2,1)} %collective-permute-done.2), channel_id=1, source_target_pairs={{248,0},{0,8},{8,16},{16,24},{24,32},{32,40},{40,48},{48,56},{56,6... | collective-permute-start | bytes 3145736 | tf_op jit(solution)/shard_map/ppermute | solution.py:12
  194.1 6.7 %copy-start.1 = (bf16[1,256,2048]{2,1,0:T(8,128)(2,1)S(1)}, bf16[1,256,2048]{2,1,0:T(8,128)(2,1)}, u32[]{:S(2)}) copy-start(bf16[1,256,2048]{2,1,0:T(8,128)(2,1)} %all-gather.5.cloned.1.call-done) | copy-start | bytes 3145732
  200.8 3.3 %copy-start = (bf16[1,512,2048]{2,1,0:T(8,128)(2,1)S(1)}, bf16[1,512,2048]{2,1,0:T(8,128)(2,1)}, u32[]{:S(2)}) copy-start(bf16[1,512,2048]{2,1,0:T(8,128)(2,1)} %all-gather.3.cloned.1.call-done) | copy-start | bytes 6291460
Sparse Core Ops, SparseCore 0:
  10.0 33.3 all-gather.2
  269.2 50.0 reduce-scatter.1
Sparse Core Ops, SparseCore 1:
  45.0 28.4 all-gather.4
where the time goes:
time: 329 us; the launch traced here: 327 us
  waiting for transfers between devices  257 us (78%)
  matrix products  38.1 us (12%)
  between operations  19.9 us (6%)
  other arithmetic  6.65 us (2%)
    ppermute x6, waiting for transfers between devices, passed_along(): return lax.ppermute(block, axis, route)  170 us
    reduce_scatter x1, waiting for transfers between devices, per_device(): return lax.psum_scatter(gradient, 'vb', scatter_dimension=1, tiled=True)  50.2 us
    all_gather x1, waiting for transfers between devices, per_device(): own_rows = lax.all_gather(aux_factors, 'vb', axis=1, tiled=True)  35.2 us
    dot_general x4, matrix products, per_device(): jnp.einsum('iajb,jbp->iap', weights, far_columns, preferred_element_type=...  28.5 us
    dot_general x3, matrix products, per_device(): jnp.einsum('ibp,jap->iajb', own_columns, far_rows, preferred_element_type...  9.59 us
    reduce_sum x3, other arithmetic, lookup(): return jnp.sum(jnp.where(matches, energies[None, :], 0.0), axis=1)  6.64 us
  transfers between devices with their start and end apart: 9, of which 7 were waited for; matrix products, arithmetic and copies ran while one was open for 12% of the time, Pallas kernels for 0%

commit v1 on v0

v1 whole, which is shorter than its diff:
```python
import functools

import jax
import jax.numpy as jnp
from jax import lax
from jax.experimental import pallas as pl
from jax.experimental.pallas import tpu as pltpu
from jax.sharding import PartitionSpec as P

MESH = pl.DeviceIdType.MESH
STEPS = 4
RING = 4
HALF = 64
QUARTER = 32
BLOCK = 128
NT = (((1,), (1,)), ((), ()))

ORDER = (
    (0, 0), (0, 3), (0, 1), (3, 0), (1, 0), (0, 2), (2, 0), (1, 3),
    (3, 3), (3, 1), (1, 1), (1, 2), (2, 3), (3, 2), (2, 1), (2, 2),
)
RELAYED = ((0, 1), (0, 0), (3, 0), (1, 0), (2, 0))


def pick(step, values):
    out = jnp.int32(values[0])
    for k, value in enumerate(values):
        if k and value != values[0]:
            out = jnp.where(step == k, jnp.int32(value), out)
    return out


def kernel(occ_count, aux, vir_e, vir_i, occ_e, occ_i, out, held, relay, acc, ev_row, ev_col,
           eo, send, recv, relay_send, relay_recv, pair_send, pair_recv, own_sem):
    occ = lax.axis_index("occ")
    va = lax.axis_index("va")
    vb = lax.axis_index("vb")
    x = va * 2 + vb // 2
    core = vb % 2
    y = occ % RING

    def at(occ_shift, x_shift=0, other_core=False):
        xs = (x + x_shift + RING) % RING
        cs = 1 - core if other_core else core
        return ((occ + occ_shift + occ_count) % occ_count, xs // 2, (xs % 2) * 2 + cs)

    peers = [at(0, 1), at(0, -1), at(1), at(-1), at(3), at(-3), at(4), at(-4), at(0, 0, True)]
    barrier = pltpu.get_barrier_semaphore()
    for peer in peers:
        pl.semaphore_signal(barrier, inc=1, device_id=peer, device_id_type=MESH)
    pl.semaphore_wait(barrier, len(peers))

    def rows(d, xr, h, q=None):
        start = h * HALF + (0 if q is None else q * QUARTER)
        return held.at[d, xr, pl.ds(start, HALF if q is None else QUARTER)]

    def own_rows(h):
        return aux.at[pl.ds(h * HALF, HALF)]

    def link(src, d, xr, h, q, whole, peer):
        return pltpu.make_async_remote_copy(
            src_ref=src, dst_ref=rows(d, xr, h, None if whole else q),
            send_sem=send.at[d, xr, h, q], recv_sem=recv.at[d, xr, h, q],
            device_id=peer, device_id_type=MESH)

    def arrived(d, xr, h):
        if d == 2 and (h == 0 or xr == 0) or xr == 2 and (h == 1 or d == 0):
            for q in range(2):
                link(rows(d, xr, h, q), d, xr, h, q, False, at(1)).wait_recv()
        else:
            link(rows(d, xr, h), d, xr, h, 0, True, at(1)).wait_recv()

    def source(d, xr, h):
        return own_rows(h) if d == 0 and xr == 0 else rows(d, xr, h)

    started = []

    def start(copy):
        copy.start()

    def send_x(d, xr, h):
        start(link(source(d, xr, h), d, 3, h, 0, True, at(0, 1)))
        start(link(source(d, xr, h), d, 1, h, 0, True, at(0, -1)))

    def relay_copy(k, src):
        return pltpu.make_async_remote_copy(
            src_ref=src, dst_ref=relay.at[k],
            send_sem=send.at[1, RELAYED[k][0], RELAYED[k][1], 0], recv_sem=relay_recv.at[k],
            device_id=at(-3), device_id_type=MESH)

    def send_y(xr, h):
        src = source(0, xr, h)
        k = RELAYED.index((xr, h))

        @pl.when(y == RING - 1)
        def _():
            relay_copy(k, src).start()

        @pl.when(y != RING - 1)
        def _():
            link(src, 1, xr, h, 0, True, at(1)).start()

        start(link(src, 3, xr, h, 0, True, at(3)))

    def relayed(k):
        xr, h = RELAYED[k]
        return pltpu.make_async_remote_copy(
            src_ref=relay.at[k], dst_ref=rows(1, xr, h),
            send_sem=relay_send.at[k], recv_sem=recv.at[1, xr, h, 0],
            device_id=at(4), device_id_type=MESH)

    def pass_relay(k):
        @pl.when(y == 0)
        def _():
            relay_copy(k, relay.at[k]).wait_recv()
            relayed(k).start()

    def x_far(d, xr, h):
        if xr == 3:
            start(link(rows(d, 3, h, 0), d, 2, h, 0, False, at(0, 1)))
        else:
            start(link(rows(d, 1, h, 1), d, 2, h, 1, False, at(0, -1)))

    def y_far(d, xr, h):
        if d == 1:
            start(link(rows(1, xr, h, 0), 2, xr, h, 0, False, at(1)))
        else:
            start(link(rows(3, xr, h, 1), 2, xr, h, 1, False, at(-1)))

    def pair(src, d, xr, h):
        return pltpu.make_async_remote_copy(
            src_ref=src, dst_ref=held.at[d, xr, pl.ds(BLOCK + h * HALF, HALF)],
            send_sem=pair_send.at[d, xr, h], recv_sem=pair_recv.at[d, xr, h],
            device_id=at(0, 0, True), device_id_type=MESH)

    def pair_start(d, xr, h):
        pair(source(d, xr, h), d, xr, h).start()

    def take(d, xr, h):
        arrived(d, xr, h)
        if h == 0:
            if d == 0:
                if xr != 2:
                    x_far(d, xr, h)
                send_y(xr, h)
            elif d != 2:
                y_far(d, xr, h)
        else:
            if xr == 0:
                if d != 2:
                    y_far(d, xr, h)
                send_x(d, xr, h)
            elif xr != 2:
                x_far(d, xr, h)
        pair_start(d, xr, h)

    def pair_ready(d, xr):
        for h in range(2):
            pair(source(d, xr, h), d, xr, h).wait_recv()

    own_copy = pltpu.make_async_copy(aux, held.at[0, 0, pl.ds(0, BLOCK)], own_sem)

    def ev_start():
        send_x(0, 0, 0)
        send_y(0, 1)
        own_copy.start()
        pair_start(0, 0, 0)
        pair_start(0, 0, 1)
        send_x(0, 0, 1)
        send_y(0, 0)

    def ev0():
        own_copy.wait()

    def ev1():
        take(0, 3, 0)
        take(0, 1, 0)
        take(3, 0, 1)
        pass_relay(0)
        take(1, 0, 1)
        take(0, 3, 1)

    def ev2():
        take(0, 1, 1)
        take(3, 0, 0)
        pass_relay(1)

    def ev3():
        take(2, 0, 1)
        take(0, 2, 0)
        take(1, 0, 0)

    def ev5():
        take(0, 2, 1)
        take(2, 0, 0)

    def ev7():
        pass_relay(2)
        take(1, 3, 1)
        take(1, 1, 1)
        take(3, 3, 0)
        take(1, 3, 0)

    def ev8():
        pass_relay(3)
        take(3, 3, 1)

    def ev9():
        take(3, 1, 1)
        take(3, 1, 0)

    def ev10():
        take(1, 1, 0)

    def ev11():
        pass_relay(4)
        take(2, 3, 1)
        take(2, 1, 1)
        take(3, 2, 0)
        take(1, 2, 0)
        take(1, 2, 1)

    def ev12():
        take(2, 3, 0)

    def ev13():
        take(3, 2, 1)

    def ev14():
        take(2, 1, 0)

    def ev15():
        take(2, 2, 0)
        take(2, 2, 1)

    events = {0: ev0, 1: ev1, 2: ev2, 3: ev3, 5: ev5, 7: ev7, 8: ev8, 9: ev9, 10: ev10, 11: ev11,
              12: ev12, 13: ev13, 14: ev14, 15: ev15}

    ev_start()

    acc[...] = jnp.zeros_like(acc)
    lookup_energies(occ, occ_count, x, core, vir_e, vir_i, occ_e, occ_i, ev_row, ev_col, eo)

    def tile(step, carry):
        for k, event in events.items():
            pl.when(step == k)(event)
        for k, (d, xr) in enumerate(ORDER):
            pl.when(step == k)(functools.partial(pair_ready, d, xr))
        d = pick(step, [o[0] for o in ORDER])
        xr = pick(step, [o[1] for o in ORDER])
        coul = lax.dot_general(held[0, 0, 0:BLOCK], held[d, xr], NT, preferred_element_type=jnp.float32)
        swap = lax.dot_general(held[d, 0, 0:BLOCK], held[0, xr], NT, preferred_element_type=jnp.float32)
        xs = (x + xr) % RING
        near = ev_row[pl.ds((xs % 2) * 4 + core * 2 + xs // 2, 1), :]
        far = ev_row[pl.ds((xs % 2) * 4 + (1 - core) * 2 + xs // 2, 1), :]
        base = eo[pl.ds(0, 1), :] + eo[pl.ds(d, 1), :]
        left = jnp.broadcast_to(base, (BLOCK, BLOCK)) - ev_col[...]
        gap = jnp.concatenate([left - near, left - far], axis=1)
        weights = ((2.0 * coul - swap) / gap).astype(jnp.bfloat16)
        for c in range(4):
            cols = pl.ds(c * 512, 512)
            acc[:, cols] += jnp.dot(weights, held[d, xr, :, cols], preferred_element_type=jnp.float32)
        return carry

    lax.fori_loop(0, len(ORDER), tile, 0)
    out[...] = acc[...]

    for d in range(STEPS):
        for xr in range(RING):
            for h in range(2):
                pair(source(d, xr, h), d, xr, h).wait_send()
                if d == 0 and xr == 0:
                    continue
                if d == 2 and (h == 0 or xr == 0) or xr == 2 and (h == 1 or d == 0):
                    for q in range(2):
                        link(rows(d, xr, h, q), d, xr, h, q, False, at(1)).wait_send()
                else:
                    link(rows(d, xr, h), d, xr, h, 0, True, at(1)).wait_send()

    @pl.when(y == 0)
    def _():
        for k in range(len(RELAYED)):
            relayed(k).wait_send()


def lookup_energies(occ, occ_count, x, core, vir_e, vir_i, occ_e, occ_i, ev_row, ev_col, eo):
    groups = vir_e.shape[0]
    lanes = lax.broadcasted_iota(jnp.int32, occ_e.shape, 1)
    for d in range(STEPS):
        mine = lanes == (occ - d + occ_count) % occ_count
        index = jnp.sum(jnp.where(mine, occ_i[...], 0), axis=1, keepdims=True)
        value = jnp.sum(jnp.where(lanes == index, occ_e[...], 0.0), axis=1, keepdims=True)
        eo[pl.ds(d, 1), :] = jnp.broadcast_to(value, (1, BLOCK))
    ev_row[...] = jnp.zeros_like(ev_row)
    place = lax.broadcasted_iota(jnp.int32, (BLOCK, BLOCK), 0)

    def group(g, carry):
        table = jnp.transpose(jnp.broadcast_to(vir_e[pl.ds(g, 1), :], (BLOCK, BLOCK)))
        for r in range(groups):
            hit = place + g * BLOCK == jnp.broadcast_to(vir_i[pl.ds(r, 1), :], (BLOCK, BLOCK))
            ev_row[pl.ds(r, 1), :] += jnp.sum(jnp.where(hit, table, 0.0), axis=0, keepdims=True)
        return carry

    lax.fori_loop(0, groups, group, 0)
    mine = ev_row[pl.ds((x % 2) * 4 + core * 2 + x // 2, 1), :]
    ev_col[...] = jnp.transpose(jnp.broadcast_to(mine, (BLOCK, BLOCK)))


def per_device(aux_factors, occ_energy, vir_energy, occ_index, vir_index):
    occ_count = lax.axis_size("occ")
    _, width, aux_width = aux_factors.shape
    groups = vir_energy.shape[0] // BLOCK
    vmem = pl.BlockSpec(memory_space=pltpu.VMEM)
    dma = pltpu.SemaphoreType.DMA
    result = pl.pallas_call(
        functools.partial(kernel, occ_count),
        out_shape=jax.ShapeDtypeStruct((width, aux_width), jnp.float32),
        in_specs=[pl.BlockSpec(memory_space=pl.ANY)] + [vmem] * 4,
        out_specs=vmem,
        scratch_shapes=[
            pltpu.VMEM((STEPS, RING, 2 * BLOCK, aux_width), jnp.bfloat16),
            pltpu.VMEM((len(RELAYED), HALF, aux_width), jnp.bfloat16),
            pltpu.VMEM((width, aux_width), jnp.float32),
            pltpu.VMEM((groups, BLOCK), jnp.float32),
            pltpu.VMEM((BLOCK, BLOCK), jnp.float32),
            pltpu.VMEM((8, BLOCK), jnp.float32),
            dma((STEPS, RING, 2, 2)),
            dma((STEPS, RING, 2, 2)),
            dma((len(RELAYED),)),
            dma((len(RELAYED),)),
            dma((STEPS, RING, 2)),
            dma((STEPS, RING, 2)),
            dma,
        ],
        compiler_params=pltpu.CompilerParams(
            collective_id=0, has_side_effects=True, vmem_limit_bytes=40 << 20),
        cost_estimate=pl.CostEstimate(
            flops=6 * STEPS * width * 8 * BLOCK * aux_width, bytes_accessed=2 << 20, transcendentals=0),
    )(
        aux_factors.reshape(width, aux_width),
        vir_energy.reshape(groups, BLOCK),
        vir_index.reshape(groups, BLOCK),
        occ_energy.reshape(1, -1),
        occ_index.reshape(1, -1),
    )
    return result.reshape(1, width, aux_width)


def solution(mesh):
    return jax.shard_map(
        per_device,
        mesh=mesh,
        in_specs=(P("occ", ("vb", "va"), None), P(), P(), P(), P()),
        out_specs=P("occ", ("vb", "va"), None),
        check_vma=False,
    )
```

time: 329 us -> 95.5 us (0.29)
  the two profiles are of different devices: /device:TPU:96 before, /device:TPU:1 now
where the time goes in v1:
time: 95.5 us; the launch traced here: 95.3 us
  Pallas kernels  92.6 us (97%)
  local copies, waits for them, and re-layouts  2.71 us (3%)
    pallas_call x1, Pallas kernels, per_device(): pl.pallas_call(functools.partial(kernel, occ_count), out_shape=jax.ShapeD...  92.6 us
    unnamed x11, local copies, waits for them, and re-layouts  2.71 us

profile of v1, /device:TPU:1, one launch (start us, length us, event | category | flops | bytes accessed | tf_op | source)
XLA Modules:
  0.0 95.3 jit_solution(7190519647527155183)
XLA Ops:
  0.0 0.0 copy-start.2
  0.0 0.0 copy-start.1
  0.0 0.0 copy-start.3
  0.0 0.0 copy-start.4
  0.0 0.7 copy-done.2
  0.7 0.0 copy-done.1
  0.7 0.0 copy-done.3
  0.7 0.0 copy-done.4
  0.7 0.0 copy-start
  0.7 1.0 %copy-done = bf16[1,128,2048]{2,1,0:T(8,128)(2,1)S(1)} copy-done((bf16[1,128,2048]{2,1,0:T(8,128)(2,1)S(1)}, bf16[1,128,2048]{2,1,0:T(8,128)(2,1)}, u32[]{:S(2)}) %copy-start) | copy-done | bytes 524312
  1.8 92.6 %shard_map.55 = f32[128,2048]{1,0:T(8,128)S(1)} custom-call(bf16[128,2048]{1,0:T(8,128)(2,1)S(1)} %bitcast.7, f32[8,128]{1,0:T(8,128)S(1)} %bitcast.8, s32[8,128]{1,0:T(8,128)S(1)} %bitcast.9, f32[1,32]{1,0:T(1,128)S(1)} %bitcast.10, s32[1,32]{1,0:T(1,128)S(1)} %bitcast.11), custom_call_target="tpu_custom_call" | custom-call | flops 6442450944 | bytes 2097152 | tf_op jit(solution)/shard_map/pallas_call | solution.py:315
  94.4 1.0 %copy.7 = f32[1,128,2048]{2,1,0:T(8,128)} copy(f32[1,128,2048]{2,1,0:T(8,128)S(1)} %bitcast.6) | data formatting | bytes 2097152
Async XLA Ops:
  0.0 0.7 copy-start.2
  0.0 0.7 copy-start.1
  0.0 0.7 copy-start.3
  0.0 0.7 copy-start.4
  0.7 1.0 %copy-start = (bf16[1,128,2048]{2,1,0:T(8,128)(2,1)S(1)}, bf16[1,128,2048]{2,1,0:T(8,128)(2,1)}, u32[]{:S(2)}) copy-start(bf16[1,128,2048]{2,1,0:T(8,128)(2,1)} %param.5) | copy-start | bytes 1572868

commit v2 on v0

v2 whole, which is shorter than its diff:
```python
import functools

import jax
import jax.numpy as jnp
from jax import lax
from jax.experimental import pallas as pl
from jax.experimental.pallas import tpu as pltpu
from jax.sharding import PartitionSpec as P

LOGICAL = pl.DeviceIdType.LOGICAL
STEPS = 4
RING = 4
BLOCK = 128
PIECES = 4
FIRST = PIECES // 2
PIECE = BLOCK // PIECES
NT = (((1,), (1,)), ((), ()))

ORDER = (
    (0, 0),
    (0, 1),
    (3, 0),
    (0, 3),
    (1, 0),
    (0, 2),
    (3, 1),
    (1, 1),
    (3, 3),
    (2, 0),
    (1, 3),
    (2, 1),
    (3, 2),
    (1, 2),
    (2, 3),
    (2, 2),
)
PLAN = (
    (),
    ((0,), (0, 1, 0), (3, 0, 2), (1,), (0, 1, 1), (0, 3, 1), (0, 1, 2), (0, 3, 2), (0, 3, 3), (3,), (0, 1, 3), (2,), (3, 0, 0), (3, 0, 3), (0, 3, 0), (1, 0, 3), (3, 0, 1), (1, 0, 2), (6,), (3, 3, 2), (3, 1, 2), (3, 1, 0), (0, 2, 2), (7,), (0, 2, 1), (1, 0, 1), (1, 0, 0)),
    ((4,), (3, 3, 3), (0, 2, 3)),
    ((3, 1, 3), (5,), (0, 2, 0), (1, 1, 0), (2, 0, 3), (9,), (1, 1, 1), (3, 1, 1)),
    ((1, 3, 3),),
    ((1, 3, 0), (2, 0, 2), (1, 1, 3), (1, 3, 2), (1, 1, 2), (2, 0, 1), (8,), (3, 3, 1)),
    ((3, 3, 0),),
    ((1, 3, 1), (3, 2, 3), (3, 2, 1), (3, 2, 2), (2, 1, 3), (2, 0, 0)),
    (),
    ((1, 2, 0), (2, 1, 2), (2, 3, 2), (2, 1, 0), (2, 1, 1), (2, 3, 3)),
    ((1, 2, 1), (3, 2, 0), (1, 2, 3), (1, 2, 2)),
    ((2, 3, 1), (2, 2, 3), (2, 3, 0)),
    ((2, 2, 1), (2, 2, 2), (2, 2, 0)),
    (),
    (),
    (),
)
RELAYED = (
    tuple((0, q) for q in range(FIRST, PIECES))
    + tuple((0, q) for q in range(FIRST))
    + tuple((xr, q) for xr in (3, 1, 2) for q in range(FIRST))
)


def pick(step, values):
    out = jnp.int32(values[0])
    for k, value in enumerate(values):
        if k and value != values[0]:
            out = jnp.where(step == k, jnp.int32(value), out)
    return out


def kernel(occ_count, aux, vir_e_in, vir_i_in, occ_e_in, occ_i_in, out, held, relay, vir_e, vir_i, occ_e, occ_i,
           ev_row, ev_col, eo, weights, send, recv, relay_send, relay_recv, pair_send, pair_recv, own_sem):
    occ = lax.axis_index("occ")
    va = lax.axis_index("va")
    vb = lax.axis_index("vb")
    x = va * 2 + vb // 2
    core = vb % 2
    y = occ % RING

    va_count = lax.axis_size("va")
    vb_count = lax.axis_size("vb")

    def device(occ_shift, x_shift=0, other_core=False):
        xs = (x + x_shift + RING) % RING
        cs = 1 - core if other_core else core
        far = (occ + occ_shift + occ_count) % occ_count
        return (far * va_count + xs // 2) * vb_count + (xs % 2) * 2 + cs

    right, left_side = device(0, 1), device(0, -1)
    ahead = {k: device(k) for k in (1, -1, 3, -3, 4, -4)}
    partner = device(0, 0, True)
    first_row = y == 0
    last_row = y == RING - 1

    tables = [
        pltpu.make_async_copy(src, dst, own_sem.at[1 + k])
        for k, (src, dst) in enumerate(((vir_e_in, vir_e), (vir_i_in, vir_i), (occ_e_in, occ_e), (occ_i_in, occ_i)))
    ]
    own_copy = pltpu.make_async_copy(aux, held.at[0, 0, pl.ds(0, BLOCK)], own_sem.at[0])
    peers = [right, left_side, *ahead.values(), partner]
    barrier = pltpu.get_barrier_semaphore()
    for peer in peers:
        pl.semaphore_signal(barrier, inc=1, device_id=peer, device_id_type=LOGICAL)
    own_copy.start()
    for table in tables:
        table.start()
    pl.semaphore_wait(barrier, len(peers))

    def rows(d, xr, q):
        return held.at[d, xr, pl.ds(q * PIECE, PIECE)]

    def source(d, xr, q):
        return aux.at[pl.ds(q * PIECE, PIECE)] if d == 0 and xr == 0 else rows(d, xr, q)

    def link(src, d, xr, q, peer):
        return pltpu.make_async_remote_copy(
            src_ref=src, dst_ref=rows(d, xr, q), send_sem=send.at[d, xr, q], recv_sem=recv.at[d, xr, q],
            device_id=peer, device_id_type=LOGICAL)

    def relay_in(k, src):
        xr, q = RELAYED[k]
        return pltpu.make_async_remote_copy(
            src_ref=src, dst_ref=relay.at[k], send_sem=send.at[1, xr, q], recv_sem=relay_recv.at[k],
            device_id=ahead[-3], device_id_type=LOGICAL)

    def relay_out(k):
        xr, q = RELAYED[k]
        return pltpu.make_async_remote_copy(
            src_ref=relay.at[k], dst_ref=rows(1, xr, q), send_sem=relay_send.at[k], recv_sem=recv.at[1, xr, q],
            device_id=ahead[4], device_id_type=LOGICAL)

    def send_x(d, q):
        link(source(d, 0, q), d, 3, q, right).start()
        link(source(d, 0, q), d, 1, q, left_side).start()

    def send_y(xr, q):
        src = source(0, xr, q)

        @pl.when(last_row)
        def _():
            relay_in(RELAYED.index((xr, q)), src).start()

        @pl.when(jnp.logical_not(last_row))
        def _():
            link(src, 1, xr, q, ahead[1]).start()

        link(src, 3, xr, q, ahead[3]).start()

    def pass_relay(k):
        @pl.when(first_row)
        def _():
            relay_in(k, relay.at[k]).wait_recv()
            relay_out(k).start()

    def x_far(d, xr, q):
        if xr == 3 and q % 2 == 0:
            link(rows(d, xr, q), d, 2, q, right).start()
        if xr == 1 and q % 2 == 1:
            link(rows(d, xr, q), d, 2, q, left_side).start()

    def y_far(d, xr, q):
        if d == 1 and q % 2 == 0:
            link(rows(d, xr, q), 2, xr, q, ahead[1]).start()
        if d == 3 and q % 2 == 1:
            link(rows(d, xr, q), 2, xr, q, ahead[-1]).start()

    def pair(d, xr, h):
        span = pl.ds(h * FIRST * PIECE, FIRST * PIECE)
        src = aux.at[span] if d == 0 and xr == 0 else held.at[d, xr, span]
        return pltpu.make_async_remote_copy(
            src_ref=src, dst_ref=held.at[d, xr, pl.ds(BLOCK + h * FIRST * PIECE, FIRST * PIECE)],
            send_sem=pair_send.at[d, xr, h], recv_sem=pair_recv.at[d, xr, h],
            device_id=partner, device_id_type=LOGICAL)

    missing = {(d, xr, h): FIRST for d in range(STEPS) for xr in range(RING) for h in range(2)}

    def take(d, xr, q):
        link(rows(d, xr, q), d, xr, q, ahead[1]).wait_recv()
        if q < FIRST:
            if d == 0:
                x_far(d, xr, q)
                send_y(xr, q)
            else:
                y_far(d, xr, q)
        elif xr == 0:
            y_far(d, xr, q)
            send_x(d, q)
        else:
            x_far(d, xr, q)
        h = q // FIRST
        missing[d, xr, h] -= 1
        if missing[d, xr, h] == 0:
            pair(d, xr, h).start()

    def pair_ready(d, xr):
        for h in range(2):
            pair(d, xr, h).wait_recv()

    def events(k):
        for item in PLAN[k]:
            if len(item) == 1:
                pass_relay(*item)
            else:
                take(*item)
        pair_ready(*ORDER[k])

    for q in range(FIRST):
        send_x(0, q)
        send_y(0, FIRST + q)
    for q in range(FIRST):
        send_x(0, FIRST + q)
        send_y(0, q)
    pair(0, 0, 0).start()
    pair(0, 0, 1).start()

    out[...] = jnp.zeros_like(out)
    for table in tables:
        table.wait()
    lookup_energies(occ, occ_count, x, core, vir_e, vir_i, occ_e, occ_i, ev_row, ev_col, eo)
    own_copy.wait()

    def tile_of(step):
        if isinstance(step, int):
            return ORDER[step]
        return pick(step, [o[0] for o in ORDER]), pick(step, [o[1] for o in ORDER])

    def add_gradient(step):
        d, xr = tile_of(step)
        held_weights = weights[...]
        for c in range(4):
            cols = pl.ds(c * 512, 512)
            out[:, cols] += jnp.dot(held_weights, held[d, xr, :, cols], preferred_element_type=jnp.float32)

    def tile(step, carry):
        for k in range(len(ORDER)):
            pl.when(step == k)(functools.partial(events, k))
        add_gradient(step - jnp.minimum(step, 1))
        d, xr = tile_of(step)
        coul = lax.dot_general(held[0, 0, 0:BLOCK], held[d, xr], NT, preferred_element_type=jnp.float32)
        swap = lax.dot_general(held[d, 0, 0:BLOCK], held[0, xr], NT, preferred_element_type=jnp.float32)
        xs = (x + xr) % RING
        near = ev_row[pl.ds((xs % 2) * 4 + core * 2 + xs // 2, 1), :]
        far = ev_row[pl.ds((xs % 2) * 4 + (1 - core) * 2 + xs // 2, 1), :]
        base = eo[pl.ds(0, 1), :] + eo[pl.ds(d, 1), :]
        left = jnp.broadcast_to(base, (BLOCK, BLOCK)) - ev_col[...]
        gap = jnp.concatenate([left - near, left - far], axis=1)
        weights[...] = ((2.0 * coul - swap) / gap).astype(jnp.bfloat16)
        return carry

    weights[...] = jnp.zeros_like(weights)
    lax.fori_loop(0, len(ORDER), tile, 0)
    add_gradient(len(ORDER) - 1)

    for d in range(STEPS):
        for xr in range(RING):
            for h in range(2):
                pair(d, xr, h).wait_send()
            if d or xr:
                for q in range(PIECES):
                    link(rows(d, xr, q), d, xr, q, ahead[1]).wait_send()

    @pl.when(first_row)
    def _():
        for k in range(len(RELAYED)):
            relay_out(k).wait_send()


def lookup_energies(occ, occ_count, x, core, vir_e, vir_i, occ_e, occ_i, ev_row, ev_col, eo):
    groups = vir_e.shape[0]
    lanes = lax.broadcasted_iota(jnp.int32, occ_e.shape, 1)
    for d in range(STEPS):
        mine = lanes == (occ - d + occ_count) % occ_count
        index = jnp.sum(jnp.where(mine, occ_i[...], 0), axis=1, keepdims=True)
        value = jnp.sum(jnp.where(lanes == index, occ_e[...], 0.0), axis=1, keepdims=True)
        eo[pl.ds(d, 1), :] = jnp.broadcast_to(value, (1, BLOCK))
    ev_row[...] = jnp.zeros_like(ev_row)
    place = lax.broadcasted_iota(jnp.int32, (BLOCK, BLOCK), 0)

    def group(g, carry):
        table = jnp.transpose(jnp.broadcast_to(vir_e[pl.ds(g, 1), :], (BLOCK, BLOCK)))
        for r in range(groups):
            hit = place + g * BLOCK == jnp.broadcast_to(vir_i[pl.ds(r, 1), :], (BLOCK, BLOCK))
            ev_row[pl.ds(r, 1), :] += jnp.sum(jnp.where(hit, table, 0.0), axis=0, keepdims=True)
        return carry

    lax.fori_loop(0, groups, group, 0)
    mine = ev_row[pl.ds((x % 2) * 4 + core * 2 + x // 2, 1), :]
    ev_col[...] = jnp.transpose(jnp.broadcast_to(mine, (BLOCK, BLOCK)))


def per_device(aux_factors, occ_energy, vir_energy, occ_index, vir_index):
    occ_count = lax.axis_size("occ")
    _, width, aux_width = aux_factors.shape
    groups = vir_energy.shape[0] // BLOCK
    dma = pltpu.SemaphoreType.DMA
    in_hbm = functools.partial(pltpu.with_memory_space_constraint, memory_space=pltpu.HBM)
    result = pl.pallas_call(
        functools.partial(kernel, occ_count),
        out_shape=jax.ShapeDtypeStruct((width, aux_width), jnp.float32),
        in_specs=[pl.BlockSpec(memory_space=pltpu.HBM)] * 5,
        out_specs=pl.BlockSpec(memory_space=pltpu.VMEM),
        scratch_shapes=[
            pltpu.VMEM((STEPS, RING, 2 * BLOCK, aux_width), jnp.bfloat16),
            pltpu.VMEM((len(RELAYED), PIECE, aux_width), jnp.bfloat16),
            pltpu.VMEM((groups, BLOCK), jnp.float32),
            pltpu.VMEM((groups, BLOCK), jnp.int32),
            pltpu.VMEM((1, occ_count), jnp.float32),
            pltpu.VMEM((1, occ_count), jnp.int32),
            pltpu.VMEM((groups, BLOCK), jnp.float32),
            pltpu.VMEM((BLOCK, BLOCK), jnp.float32),
            pltpu.VMEM((8, BLOCK), jnp.float32),
            pltpu.VMEM((BLOCK, 2 * BLOCK), jnp.bfloat16),
            dma((STEPS, RING, PIECES)),
            dma((STEPS, RING, PIECES)),
            dma((len(RELAYED),)),
            dma((len(RELAYED),)),
            dma((STEPS, RING, 2)),
            dma((STEPS, RING, 2)),
            dma((5,)),
        ],
        compiler_params=pltpu.CompilerParams(
            collective_id=0, has_side_effects=True, vmem_limit_bytes=40 << 20),
        cost_estimate=pl.CostEstimate(
            flops=6 * STEPS * width * 8 * BLOCK * aux_width, bytes_accessed=2 << 20, transcendentals=0),
    )(
        in_hbm(aux_factors.reshape(width, aux_width)),
        in_hbm(vir_energy.reshape(groups, BLOCK)),
        in_hbm(vir_index.reshape(groups, BLOCK)),
        in_hbm(occ_energy.reshape(1, occ_count)),
        in_hbm(occ_index.reshape(1, occ_count)),
    )
    return result.reshape(1, width, aux_width)


def solution(mesh):
    return jax.shard_map(
        per_device,
        mesh=mesh,
        in_specs=(P("occ", ("vb", "va"), None), P(), P(), P(), P()),
        out_specs=P("occ", ("vb", "va"), None),
        check_vma=False,
    )
```

time: 329 us -> 67.2 us (0.20)
  waiting for transfers between devices: 257 us -> 0 us
  Pallas kernels: 0 us -> 66.1 us
  matrix products: 38.1 us -> 0 us
  between operations: 19.9 us -> 0.01 us
  other arithmetic: 6.65 us -> 0 us
    ppermute x6 -> x0, waiting for transfers between devices: 170 us -> none  [passed_along(): return lax.ppermute(block, axis, route)]
    pallas_call x0 -> x1, Pallas kernels: none -> 66.1 us  [per_device(): pl.pallas_call(functools.partial(kernel, occ_count), out_shape=jax.ShapeD...]
    reduce_scatter x1 -> x0, waiting for transfers between devices: 50.2 us -> none  [per_device(): return lax.psum_scatter(gradient, 'vb', scatter_dimension=1, tiled=True)]
    dot_general x7 -> x0, matrix products: 38.1 us -> none  [the longest x4 28.5 us: per_device(): jnp.einsum('iajb,jbp->iap', weights, far_columns, preferred_element_type=...]
    all_gather x2 -> x0, waiting for transfers between devices: 35.2 us -> none  [the longest x1 35.2 us: per_device(): own_rows = lax.all_gather(aux_factors, 'vb', axis=1, tiled=True)]
    reduce_sum x3 -> x0, other arithmetic: 6.64 us -> none  [lookup(): return jnp.sum(jnp.where(matches, energies[None, :], 0.0), axis=1)]
  transfers between devices with their start and end apart: 9 -> 0, of which waited for: 7 -> 0; matrix products, arithmetic and copies ran while one was open for 12% -> 0% of each run, Pallas kernels for 0% -> 0%
where the time goes in v2:
time: 67.2 us; the launch traced here: 67.1 us
  Pallas kernels  66.1 us (98%)
  local copies, waits for them, and re-layouts  0.97 us (1%)
    pallas_call x1, Pallas kernels, per_device(): pl.pallas_call(functools.partial(kernel, occ_count), out_shape=jax.ShapeD...  66.1 us

profile of v2, /device:TPU:96, one launch (start us, length us, event | category | flops | bytes accessed | tf_op | source)
XLA Modules:
  0.0 67.1 jit_solution(14235075541099185854)
XLA Ops:
  0.0 66.1 %shard_map.55 = f32[128,2048]{1,0:T(8,128)S(1)} custom-call(bf16[128,2048]{1,0:T(8,128)(2,1)} %bitcast.7, f32[8,128]{1,0:T(8,128)} %bitcast.8, s32[8,128]{1,0:T(8,128)} %bitcast.9, f32[1,32]{1,0:T(1,128)} %bitcast.10, s32[1,32]{1,0:T(1,128)} %bitcast.11), custom_call_target="tpu_custom_call" | custom-call | flops 6442450944 | bytes 2097152 | tf_op jit(solution)/shard_map/pallas_call | solution.py:296
  66.1 1.0 %copy.7 = f32[1,128,2048]{2,1,0:T(8,128)} copy(f32[1,128,2048]{2,1,0:T(8,128)S(1)} %bitcast.6) | data formatting | bytes 2097152

commit v3 on v2

--- a/solution.py
+++ b/solution.py
@@ -17,37 +17,37 @@
 NT = (((1,), (1,)), ((), ()))
 
 ORDER = (
+    (0, 1),
     (0, 0),
-    (0, 1),
     (3, 0),
+    (1, 0),
+    (3, 1),
     (0, 3),
-    (1, 0),
+    (3, 3),
+    (1, 3),
+    (1, 1),
     (0, 2),
-    (3, 1),
-    (1, 1),
-    (3, 3),
     (2, 0),
-    (1, 3),
-    (2, 1),
     (3, 2),
     (1, 2),
+    (2, 1),
     (2, 3),
     (2, 2),
 )
 PLAN = (
-    (),
-    ((0,), (0, 1, 0), (3, 0, 2), (1,), (0, 1, 1), (0, 3, 1), (0, 1, 2), (0, 3, 2), (0, 3, 3), (3,), (0, 1, 3), (2,), (3, 0, 0), (3, 0, 3), (0, 3, 0), (1, 0, 3), (3, 0, 1), (1, 0, 2), (6,), (3, 3, 2), (3, 1, 2), (3, 1, 0), (0, 2, 2), (7,), (0, 2, 1), (1, 0, 1), (1, 0, 0)),
-    ((4,), (3, 3, 3), (0, 2, 3)),
-    ((3, 1, 3), (5,), (0, 2, 0), (1, 1, 0), (2, 0, 3), (9,), (1, 1, 1), (3, 1, 1)),
-    ((1, 3, 3),),
-    ((1, 3, 0), (2, 0, 2), (1, 1, 3), (1, 3, 2), (1, 1, 2), (2, 0, 1), (8,), (3, 3, 1)),
-    ((3, 3, 0),),
-    ((1, 3, 1), (3, 2, 3), (3, 2, 1), (3, 2, 2), (2, 1, 3), (2, 0, 0)),
-    (),
-    ((1, 2, 0), (2, 1, 2), (2, 3, 2), (2, 1, 0), (2, 1, 1), (2, 3, 3)),
-    ((1, 2, 1), (3, 2, 0), (1, 2, 3), (1, 2, 2)),
-    ((2, 3, 1), (2, 2, 3), (2, 3, 0)),
-    ((2, 2, 1), (2, 2, 2), (2, 2, 0)),
+    (("T", 0, 3, 0), ("T", 0, 1, 0), ("R", 0), ("T", 3, 0, 2), ("XF", 0, 3, 0), ("T", 0, 1, 1), ("Y", 3, 0), ("R", 1), ("R", 2), ("Y", 1, 1), ("T", 3, 0, 3), ("XF", 0, 1, 1), ("T", 1, 0, 2), ("R", 3), ("YF", 1, 0, 2), ("T", 0, 3, 1), ("Y", 3, 1), ("T", 3, 0, 0), ("T", 0, 1, 2), ("T", 0, 1, 3), ("X", 3, 2), ("T", 0, 3, 3), ("T", 0, 3, 2), ("XF", 0, 3, 2), ("T", 1, 0, 3), ("X", 3, 3), ("R", 4), ("YF", 3, 0, 3), ("T", 3, 0, 1), ("T", 0, 2, 0), ("X", 1, 3), ("T", 3, 3, 0), ("T", 1, 0, 0), ("R", 7), ("Y", 1, 0), ("T", 3, 3, 2), ("X", 1, 2), ("Y", 2, 0), ("T", 3, 1, 2), ("T", 1, 3, 0), ("T", 1, 0, 1), ("R", 5), ("T", 3, 1, 1), ("XF", 0, 1, 3), ("R", 6), ("XF", 3, 3, 2), ("T", 0, 2, 1), ("T", 0, 2, 2), ("Y", 2, 1), ("T", 3, 1, 3), ("T", 1, 1, 1), ("T", 3, 3, 3), ("T", 1, 1, 3), ("T", 3, 3, 1)),
+    (("XF", 3, 1, 3), ("T", 1, 1, 2), ("YF", 1, 0, 0), ("T", 2, 0, 3), ("T", 2, 0, 2)),
+    (("X", 2, 2), ("T", 3, 1, 0), ("YF", 3, 0, 1), ("R", 8)),
+    (("T", 1, 3, 2), ("X", 2, 3), ("T", 0, 2, 3)),
+    (("YF", 3, 1, 1), ("T", 1, 3, 1), ("R", 9), ("XF", 1, 1, 3), ("T", 1, 1, 0), ("T", 3, 2, 0), ("YF", 1, 1, 0), ("YF", 1, 3, 0), ("T", 3, 2, 3), ("T", 1, 3, 3), ("YF", 3, 3, 1), ("XF", 1, 3, 2)),
+    (("T", 3, 2, 1), ("T", 3, 2, 2)),
+    (("T", 1, 2, 0), ("T", 2, 1, 2), ("YF", 1, 2, 0), ("T", 2, 3, 2), ("XF", 2, 3, 2), ("YF", 3, 2, 1), ("T", 2, 0, 0), ("T", 2, 0, 1)),
+    (),
+    (("T", 2, 1, 3), ("T", 1, 2, 1), ("XF", 2, 1, 3), ("T", 2, 1, 0)),
+    (),
+    (("T", 2, 1, 1), ("T", 1, 2, 3), ("T", 1, 2, 2), ("T", 2, 3, 3)),
+    (("T", 2, 3, 0), ("T", 2, 3, 1)),
+    (("T", 2, 2, 1), ("T", 2, 2, 2), ("T", 2, 2, 3), ("T", 2, 2, 0)),
     (),
     (),
     (),
@@ -68,7 +68,7 @@
 
 
 def kernel(occ_count, aux, vir_e_in, vir_i_in, occ_e_in, occ_i_in, out, held, relay, vir_e, vir_i, occ_e, occ_i,
-           ev_row, ev_col, eo, weights, send, recv, relay_send, relay_recv, pair_send, pair_recv, own_sem):
+           ev_row, ev_col, eo, weights, mine, swaps, send, recv, relay_send, relay_recv, pair_send, pair_recv, own_sem, mine_sem):
     occ = lax.axis_index("occ")
     va = lax.axis_index("va")
     vb = lax.axis_index("vb")
@@ -96,11 +96,13 @@
         for k, (src, dst) in enumerate(((vir_e_in, vir_e), (vir_i_in, vir_i), (occ_e_in, occ_e), (occ_i_in, occ_i)))
     ]
     own_copy = pltpu.make_async_copy(aux, held.at[0, 0, pl.ds(0, BLOCK)], own_sem.at[0])
+    first_mine = pltpu.make_async_copy(aux, mine.at[pl.ds(0, BLOCK)], own_sem.at[5])
     peers = [right, left_side, *ahead.values(), partner]
     barrier = pltpu.get_barrier_semaphore()
     for peer in peers:
         pl.semaphore_signal(barrier, inc=1, device_id=peer, device_id_type=LOGICAL)
     own_copy.start()
+    first_mine.start()
     for table in tables:
         table.start()
     pl.semaphore_wait(barrier, len(peers))
@@ -175,32 +177,32 @@
 
     def take(d, xr, q):
         link(rows(d, xr, q), d, xr, q, ahead[1]).wait_recv()
-        if q < FIRST:
-            if d == 0:
-                x_far(d, xr, q)
-                send_y(xr, q)
-            else:
-                y_far(d, xr, q)
-        elif xr == 0:
-            y_far(d, xr, q)
-            send_x(d, q)
-        else:
-            x_far(d, xr, q)
         h = q // FIRST
         missing[d, xr, h] -= 1
         if missing[d, xr, h] == 0:
             pair(d, xr, h).start()
+            if d % 2 and xr == 0 and missing[d, 0, 1 - h] == 0:
+                mine_copy(1 + d // 2).start()
+
+    def mine_copy(k):
+        return pltpu.make_async_copy(
+            held.at[(0, 1, 3)[k], 0, pl.ds(0, BLOCK)], mine.at[pl.ds(k * BLOCK, BLOCK)], mine_sem.at[k])
+
+    waited = []
 
     def pair_ready(d, xr):
         for h in range(2):
             pair(d, xr, h).wait_recv()
+        if not waited:
+            waited.append(True)
+            mine_copy(1).wait()
+            mine_copy(2).wait()
+
+    actions = {"T": take, "R": pass_relay, "X": send_x, "Y": send_y, "XF": x_far, "YF": y_far}
 
     def events(k):
-        for item in PLAN[k]:
-            if len(item) == 1:
-                pass_relay(*item)
-            else:
-                take(*item)
+        for what, *item in PLAN[k]:
+            actions[what](*item)
         pair_ready(*ORDER[k])
 
     for q in range(FIRST):
@@ -217,6 +219,7 @@
         table.wait()
     lookup_energies(occ, occ_count, x, core, vir_e, vir_i, occ_e, occ_i, ev_row, ev_col, eo)
     own_copy.wait()
+    first_mine.wait()
 
     def tile_of(step):
         if isinstance(step, int):
@@ -230,20 +233,45 @@
             cols = pl.ds(c * 512, 512)
             out[:, cols] += jnp.dot(held_weights, held[d, xr, :, cols], preferred_element_type=jnp.float32)
 
-    def tile(step, carry):
-        for k in range(len(ORDER)):
-            pl.when(step == k)(functools.partial(events, k))
-        add_gradient(step - jnp.minimum(step, 1))
-        d, xr = tile_of(step)
-        coul = lax.dot_general(held[0, 0, 0:BLOCK], held[d, xr], NT, preferred_element_type=jnp.float32)
-        swap = lax.dot_general(held[d, 0, 0:BLOCK], held[0, xr], NT, preferred_element_type=jnp.float32)
+    def gap_of(d, xr):
         xs = (x + xr) % RING
         near = ev_row[pl.ds((xs % 2) * 4 + core * 2 + xs // 2, 1), :]
         far = ev_row[pl.ds((xs % 2) * 4 + (1 - core) * 2 + xs // 2, 1), :]
         base = eo[pl.ds(0, 1), :] + eo[pl.ds(d, 1), :]
         left = jnp.broadcast_to(base, (BLOCK, BLOCK)) - ev_col[...]
-        gap = jnp.concatenate([left - near, left - far], axis=1)
-        weights[...] = ((2.0 * coul - swap) / gap).astype(jnp.bfloat16)
+        return jnp.concatenate([left - near, left - far], axis=1)
+
+    def product(left, d, xr):
+        return lax.dot_general(left, held[d, xr], NT, preferred_element_type=jnp.float32)
+
+    def tile(step, carry):
+        for k in range(len(ORDER)):
+            pl.when(step == k)(functools.partial(events, k))
+        before = step - jnp.minimum(step, 1)
+        d, xr = tile_of(step)
+
+        @pl.when(d == 0)
+        def _():
+            add_gradient(before)
+            coul = product(mine[...], 0, xr)
+            swaps[0, xr] = coul[BLOCK:2 * BLOCK]
+            swaps[1, xr] = coul[2 * BLOCK:]
+            coul = coul[:BLOCK]
+            weights[...] = ((2.0 * coul - coul) / gap_of(0, xr)).astype(jnp.bfloat16)
+
+        @pl.when(d % 2 == 1)
+        def _():
+            add_gradient(before)
+            coul = product(mine[0:BLOCK], d, xr)
+            weights[...] = ((2.0 * coul - swaps[d // 2, xr]) / gap_of(d, xr)).astype(jnp.bfloat16)
+
+        @pl.when(d == 2)
+        def _():
+            add_gradient(before)
+            coul = product(mine[0:BLOCK], d, xr)
+            swap = product(held[2, 0, 0:BLOCK], 0, xr)
+            weights[...] = ((2.0 * coul - swap) / gap_of(d, xr)).astype(jnp.bfloat16)
+
         return carry
 
     weights[...] = jnp.zeros_like(weights)
@@ -309,13 +337,16 @@
             pltpu.VMEM((BLOCK, BLOCK), jnp.float32),
             pltpu.VMEM((8, BLOCK), jnp.float32),
             pltpu.VMEM((BLOCK, 2 * BLOCK), jnp.bfloat16),
+            pltpu.VMEM((3 * BLOCK, aux_width), jnp.bfloat16),
+            pltpu.VMEM((2, RING, BLOCK, 2 * BLOCK), jnp.float32),
             dma((STEPS, RING, PIECES)),
             dma((STEPS, RING, PIECES)),
             dma((len(RELAYED),)),
             dma((len(RELAYED),)),
             dma((STEPS, RING, 2)),
             dma((STEPS, RING, 2)),
-            dma((5,)),
+            dma((6,)),
+            dma((3,)),
         ],
         compiler_params=pltpu.CompilerParams(
             collective_id=0, has_side_effects=True, vmem_limit_bytes=40 << 20),

time: 67.2 us -> 65.8 us (0.979)
  Pallas kernels: 66.1 us -> 64.8 us
    pallas_call x1, Pallas kernels: 66.1 us -> 64.8 us  [per_device(): pl.pallas_call(functools.partial(kernel, occ_count), out_shape=jax.ShapeD...]
where the time goes in v3:
time: 65.8 us
  Pallas kernels  64.8 us (98%)
  local copies, waits for them, and re-layouts  0.97 us (1%)
    pallas_call x1, Pallas kernels, per_device(): pl.pallas_call(functools.partial(kernel, occ_count), out_shape=jax.ShapeD...  64.8 us

profile of v3, /device:TPU:96, one launch (start us, length us, event | category | flops | bytes accessed | tf_op | source)
XLA Modules:
  0.0 65.8 jit_solution(298802188884777344)
XLA Ops:
  0.0 64.8 %shard_map.55 = f32[128,2048]{1,0:T(8,128)S(1)} custom-call(bf16[128,2048]{1,0:T(8,128)(2,1)} %bitcast.7, f32[8,128]{1,0:T(8,128)} %bitcast.8, s32[8,128]{1,0:T(8,128)} %bitcast.9, f32[1,32]{1,0:T(1,128)} %bitcast.10, s32[1,32]{1,0:T(1,128)} %bitcast.11), custom_call_target="tpu_custom_call" | custom-call | flops 6442450944 | bytes 2097152 | tf_op jit(solution)/shard_map/pallas_call | solution.py:324
  64.8 1.0 %copy.7 = f32[1,128,2048]{2,1,0:T(8,128)} copy(f32[1,128,2048]{2,1,0:T(8,128)S(1)} %bitcast.6) | data formatting | bytes 2097152

commit v4 on v3

--- a/solution.py
+++ b/solution.py
@@ -97,7 +97,7 @@
     ]
     own_copy = pltpu.make_async_copy(aux, held.at[0, 0, pl.ds(0, BLOCK)], own_sem.at[0])
     first_mine = pltpu.make_async_copy(aux, mine.at[pl.ds(0, BLOCK)], own_sem.at[5])
-    peers = [right, left_side, *ahead.values(), partner]
+    peers = [*ahead.values(), right, left_side, partner]
     barrier = pltpu.get_barrier_semaphore()
     for peer in peers:
         pl.semaphore_signal(barrier, inc=1, device_id=peer, device_id_type=LOGICAL)
@@ -204,13 +204,15 @@
         for what, *item in PLAN[k]:
             actions[what](*item)
         pair_ready(*ORDER[k])
+        if k == [o[0] for o in ORDER].index(2):
+            lax.fori_loop(0, RING, swap_at_two, 0)
 
     for q in range(FIRST):
+        send_y(0, FIRST + q)
         send_x(0, q)
-        send_y(0, FIRST + q)
     for q in range(FIRST):
+        send_y(0, q)
         send_x(0, FIRST + q)
-        send_y(0, q)
     pair(0, 0, 0).start()
     pair(0, 0, 1).start()
 
@@ -244,6 +246,10 @@
     def product(left, d, xr):
         return lax.dot_general(left, held[d, xr], NT, preferred_element_type=jnp.float32)
 
+    def swap_at_two(xr, carry):
+        swaps[2, xr] = product(held[2, 0, 0:BLOCK], 0, xr)
+        return carry
+
     def tile(step, carry):
         for k in range(len(ORDER)):
             pl.when(step == k)(functools.partial(events, k))
@@ -259,17 +265,11 @@
             coul = coul[:BLOCK]
             weights[...] = ((2.0 * coul - coul) / gap_of(0, xr)).astype(jnp.bfloat16)
 
-        @pl.when(d % 2 == 1)
+        @pl.when(d != 0)
         def _():
             add_gradient(before)
             coul = product(mine[0:BLOCK], d, xr)
-            weights[...] = ((2.0 * coul - swaps[d // 2, xr]) / gap_of(d, xr)).astype(jnp.bfloat16)
-
-        @pl.when(d == 2)
-        def _():
-            add_gradient(before)
-            coul = product(mine[0:BLOCK], d, xr)
-            swap = product(held[2, 0, 0:BLOCK], 0, xr)
+            swap = swaps[jnp.where(d == 2, 2, d // 2), xr]
             weights[...] = ((2.0 * coul - swap) / gap_of(d, xr)).astype(jnp.bfloat16)
 
         return carry
@@ -338,7 +338,7 @@
             pltpu.VMEM((8, BLOCK), jnp.float32),
             pltpu.VMEM((BLOCK, 2 * BLOCK), jnp.bfloat16),
             pltpu.VMEM((3 * BLOCK, aux_width), jnp.bfloat16),
-            pltpu.VMEM((2, RING, BLOCK, 2 * BLOCK), jnp.float32),
+            pltpu.VMEM((3, RING, BLOCK, 2 * BLOCK), jnp.float32),
             dma((STEPS, RING, PIECES)),
             dma((STEPS, RING, PIECES)),
             dma((len(RELAYED),)),

time: 65.8 us -> 66.5 us (1.011)
  no operation moved by 1% of the time
where the time goes in v4:
time: 66.5 us; the launch traced here: 66.4 us
  Pallas kernels  65.4 us (98%)
  local copies, waits for them, and re-layouts  0.97 us (1%)
    pallas_call x1, Pallas kernels, per_device(): pl.pallas_call(functools.partial(kernel, occ_count), out_shape=jax.ShapeD...  65.4 us

profile of v4, /device:TPU:96, one launch (start us, length us, event | category | flops | bytes accessed | tf_op | source)
XLA Modules:
  0.0 66.4 jit_solution(11213857258226725064)
XLA Ops:
  0.0 65.4 %shard_map.55 = f32[128,2048]{1,0:T(8,128)S(1)} custom-call(bf16[128,2048]{1,0:T(8,128)(2,1)} %bitcast.7, f32[8,128]{1,0:T(8,128)} %bitcast.8, s32[8,128]{1,0:T(8,128)} %bitcast.9, f32[1,32]{1,0:T(1,128)} %bitcast.10, s32[1,32]{1,0:T(1,128)} %bitcast.11), custom_call_target="tpu_custom_call" | custom-call | flops 6442450944 | bytes 2097152 | tf_op jit(solution)/shard_map/pallas_call | solution.py:324
  65.4 1.0 %copy.7 = f32[1,128,2048]{2,1,0:T(8,128)} copy(f32[1,128,2048]{2,1,0:T(8,128)S(1)} %bitcast.6) | data formatting | bytes 2097152

commit v5 on v3

--- a/solution.py
+++ b/solution.py
@@ -97,7 +97,7 @@
     ]
     own_copy = pltpu.make_async_copy(aux, held.at[0, 0, pl.ds(0, BLOCK)], own_sem.at[0])
     first_mine = pltpu.make_async_copy(aux, mine.at[pl.ds(0, BLOCK)], own_sem.at[5])
-    peers = [right, left_side, *ahead.values(), partner]
+    peers = [*ahead.values(), right, left_side, partner]
     barrier = pltpu.get_barrier_semaphore()
     for peer in peers:
         pl.semaphore_signal(barrier, inc=1, device_id=peer, device_id_type=LOGICAL)
@@ -206,11 +206,11 @@
         pair_ready(*ORDER[k])
 
     for q in range(FIRST):
+        send_y(0, FIRST + q)
         send_x(0, q)
-        send_y(0, FIRST + q)
     for q in range(FIRST):
+        send_y(0, q)
         send_x(0, FIRST + q)
-        send_y(0, q)
     pair(0, 0, 0).start()
     pair(0, 0, 1).start()
 

time: 65.8 us -> 65.8 us (level)
  no operation moved by 1% of the time
where the time goes in v5:
time: 65.8 us
  Pallas kernels  64.8 us (98%)
  local copies, waits for them, and re-layouts  0.97 us (1%)
    pallas_call x1, Pallas kernels, per_device(): pl.pallas_call(functools.partial(kernel, occ_count), out_shape=jax.ShapeD...  64.8 us

profile of v5, /device:TPU:96, one launch (start us, length us, event | category | flops | bytes accessed | tf_op | source)
XLA Modules:
  0.0 65.8 jit_solution(15962293850951103534)
XLA Ops:
  0.0 64.8 %shard_map.55 = f32[128,2048]{1,0:T(8,128)S(1)} custom-call(bf16[128,2048]{1,0:T(8,128)(2,1)} %bitcast.7, f32[8,128]{1,0:T(8,128)} %bitcast.8, s32[8,128]{1,0:T(8,128)} %bitcast.9, f32[1,32]{1,0:T(1,128)} %bitcast.10, s32[1,32]{1,0:T(1,128)} %bitcast.11), custom_call_target="tpu_custom_call" | custom-call | flops 6442450944 | bytes 2097152 | tf_op jit(solution)/shard_map/pallas_call | solution.py:324
  64.8 1.0 %copy.7 = f32[1,128,2048]{2,1,0:T(8,128)} copy(f32[1,128,2048]{2,1,0:T(8,128)S(1)} %bitcast.6) | data formatting | bytes 2097152
